TPU v7x, 32 devices: a whole 2x2x4 slice. The times are simulated.
32 devices in a mesh: dp: 2 (over y), ctx: 4 (over x, core), tensor: 4 (over z).
Axes of the slice: x: 2, y: 2, z: 4, core: 2. Of those that a mesh axis runs over, the one named last changes fastest.
Arguments:
- hidden: bfloat16 [4, 1024, 2048], P('dp', 'ctx'), may hold values from -6 to 6
- cotangent: bfloat16 [4, 1024, 2048], P('dp', 'ctx'), may hold values from -6 to 6
- segment_ids: int32 [4, 1024], P('dp', 'ctx'), may hold values from 0 to 5, never falling along the last dimension, each value on 1 to 800 neighbouring positions
- attn_gain: bfloat16 [2048], P(('dp', 'ctx')), may hold values from 0.5 to 1.5
- w_query: bfloat16 [2048, 2048], P(('dp', 'ctx'), 'tensor'), may hold values from -0.125 to 0.125
- key_matrix: bfloat16 [2048, 256], P(('dp', 'ctx'), 'tensor'), may hold values from -0.125 to 0.125
- value_matrix: bfloat16 [2048, 256], P(('dp', 'ctx'), 'tensor'), may hold values from -0.125 to 0.125
- w_out: bfloat16 [2048, 2048], P('tensor', ('dp', 'ctx')), may hold values from -1 to 1
- mlp_gain: bfloat16 [2048], P(('dp', 'ctx')), may hold values from 0.5 to 1.5
- w_gate: bfloat16 [2048, 5632], P(('dp', 'ctx'), 'tensor'), may hold values from -0.125 to 0.125
- w_up: bfloat16 [2048, 5632], P(('dp', 'ctx'), 'tensor'), may hold values from -0.125 to 0.125
- w_down: bfloat16 [5632, 2048], P('tensor', ('dp', 'ctx')), may hold values from -0.078125 to 0.078125
Outputs:
- layer_out: bfloat16 [4, 1024, 2048], P('dp', 'ctx')
- d_hidden: float32 [4, 1024, 2048], P('dp', 'ctx')
- grad_attn_gain: float32 [2048], P(('dp', 'ctx'))
- grad_query: float32 [2048, 2048], P(('dp', 'ctx'), 'tensor')
- grad_key: float32 [2048, 256], P(('dp', 'ctx'), 'tensor')
- grad_value: float32 [2048, 256], P(('dp', 'ctx'), 'tensor')
- grad_out: float32 [2048, 2048], P('tensor', ('dp', 'ctx'))
- grad_mlp_gain: float32 [2048], P(('dp', 'ctx'))
- grad_gate: float32 [2048, 5632], P(('dp', 'ctx'), 'tensor')
- grad_up: float32 [2048, 5632], P(('dp', 'ctx'), 'tensor')
- grad_down: float32 [5632, 2048], P('tensor', ('dp', 'ctx'))
Inputs may be any that keep to these rules, and one draw needn't show every extreme that they name: `segment_ids`: along each sequence the ids never fall, every id appears, each document holds 1 to 800 tokens, and one holds exactly 800.
All inputs are finite; a program needn't handle non-finite values.
Results may differ from a plain program's by a relative error of at most 0.013.
Values may be sent and summed in bfloat16 or wider, within the bound.
No kernel may reach another device: no remote copies, remote signals or barrier semaphores. Data moves between devices by JAX's collectives and lax.ppermute only.
A program may use at most 192 MiB of HBM per device.

v0:
```python
import jax
import jax.numpy as jnp
from jax import lax
from jax.sharding import PartitionSpec as P

MB = 2
EPSILON = 1e-05
THETA = 10000.0
NEG_FILL = -1e30


def inv_rms(values):
    return lax.rsqrt(jnp.mean(values * values, axis=-1, keepdims=True) + EPSILON)


def angles_for(positions, head_size):
    freq_index = jnp.arange(head_size // 2, dtype=jnp.float32)
    inverse = jnp.power(jnp.float32(THETA), -2.0 * freq_index / head_size)
    angle_table = positions.astype(jnp.float32)[:, None] * inverse[None, :]
    return (jnp.cos(angle_table), jnp.sin(angle_table))


def rotary(vectors, cosine, sine_table):
    half_size = vectors.shape[-1] // 2
    front_half = vectors[..., :half_size]
    back_half = vectors[..., half_size:]
    return jnp.concatenate(
        [
            front_half * cosine - back_half * sine_table,
            back_half * cosine + front_half * sine_table,
        ],
        axis=-1,
    )


def norm_back(grad_normed, source, inv_scale, gain_full):
    normalized = source * inv_scale
    scaled = grad_normed * gain_full
    middle = jnp.mean(scaled * normalized, axis=-1, keepdims=True)
    gain_term = jnp.sum(grad_normed * normalized, axis=(0, 1))
    return (inv_scale * (scaled - normalized * middle), gain_term)


def collect(shards):
    return (
        lax.all_gather(shards[0], ("dp", "ctx"), axis=0, tiled=True),
        lax.all_gather(shards[1], ("dp", "ctx"), axis=0, tiled=True),
        lax.all_gather(shards[2], ("dp", "ctx"), axis=0, tiled=True),
        lax.all_gather(shards[3], ("dp", "ctx"), axis=0, tiled=True),
        lax.all_gather(shards[4], ("dp", "ctx"), axis=1, tiled=True),
        lax.all_gather(shards[5], ("dp", "ctx"), axis=0, tiled=True),
        lax.all_gather(shards[6], ("dp", "ctx"), axis=0, tiled=True),
        lax.all_gather(shards[7], ("dp", "ctx"), axis=0, tiled=True),
        lax.all_gather(shards[8], ("dp", "ctx"), axis=1, tiled=True),
    )


def contract(left_side, right_side):
    return jnp.einsum("stc,stf->cf", left_side, right_side, preferred_element_type=jnp.float32)


def project_back(grad_rows, weight_full):
    return jnp.einsum("stf,cf->stc", grad_rows, weight_full, preferred_element_type=jnp.float32)


def per_device(
    hidden,
    cotangent,
    segment_ids,
    attn_gain,
    w_query,
    key_matrix,
    value_matrix,
    w_out,
    mlp_gain,
    w_gate,
    w_up,
    w_down,
):
    shards = (attn_gain, w_query, key_matrix, value_matrix, w_out, mlp_gain, w_gate, w_up, w_down)
    span_len = hidden.shape[1]
    model_width = hidden.shape[2]
    seq_count = hidden.shape[0] // MB
    head_size = key_matrix.shape[1]
    local_heads = w_query.shape[1] // head_size
    seq_len = span_len * lax.axis_size("ctx")
    score_scale = head_size ** (-0.5)
    positions_q = lax.axis_index("ctx") * span_len + jnp.arange(span_len, dtype=jnp.int32)
    positions_k = jnp.arange(seq_len, dtype=jnp.int32)
    cosine, sine_table = angles_for(positions_q, head_size)
    cos_heads = cosine[:, None, :]
    sin_heads = sine_table[:, None, :]
    causal = positions_q[:, None] >= positions_k[None, :]
    grad_list = [
        jnp.zeros((model_width,), jnp.float32),
        jnp.zeros((model_width, w_query.shape[1]), jnp.float32),
        jnp.zeros((model_width, key_matrix.shape[1]), jnp.float32),
        jnp.zeros((model_width, value_matrix.shape[1]), jnp.float32),
        jnp.zeros((w_out.shape[0], model_width), jnp.float32),
        jnp.zeros((model_width,), jnp.float32),
        jnp.zeros((model_width, w_gate.shape[1]), jnp.float32),
        jnp.zeros((model_width, w_up.shape[1]), jnp.float32),
        jnp.zeros((w_down.shape[0], model_width), jnp.float32),
    ]
    outputs = []
    input_grads = []
    for batch_index in range(MB):
        gathered = collect(shards)
        gain_one, query_w, key_w, value_w, out_w, gain_two, gate_w, up_w, down_w = gathered
        gain_one = gain_one.astype(jnp.float32)
        gain_two = gain_two.astype(jnp.float32)
        row_range = slice(batch_index * seq_count, (batch_index + 1) * seq_count)
        source = hidden[row_range].astype(jnp.float32)
        seg_local = segment_ids[row_range]
        inv_one = inv_rms(source)
        first_normalized = (source * inv_one * gain_one).astype(jnp.bfloat16)
        query_proj = jnp.dot(first_normalized, query_w, preferred_element_type=jnp.float32)
        projected_keys = jnp.dot(first_normalized, key_w, preferred_element_type=jnp.float32)
        projected_values = jnp.dot(first_normalized, value_w, preferred_element_type=jnp.float32)
        query_rows = rotary(
            query_proj.reshape(seq_count, span_len, local_heads, head_size), cos_heads, sin_heads
        ).astype(jnp.bfloat16)
        keys_local = rotary(projected_keys, cosine, sine_table).astype(jnp.bfloat16)
        values_local = projected_values.astype(jnp.bfloat16)
        keys_all, values_all, seg_all = (
            lax.all_gather(keys_local, "ctx", axis=1, tiled=True),
            lax.all_gather(values_local, "ctx", axis=1, tiled=True),
            lax.all_gather(seg_local.astype(jnp.bfloat16), "ctx", axis=1, tiled=True),
        )
        allowed = (seg_local[:, :, None] == seg_all.astype(jnp.int32)[:, None, :]) & causal[None]
        allowed = allowed[:, None]
        logits = (
            jnp.einsum("sqhd,skd->shqk", query_rows, keys_all, preferred_element_type=jnp.float32)
            * score_scale
        )
        logits = jnp.where(allowed, logits, NEG_FILL)
        row_peak = jnp.max(logits, axis=-1, keepdims=True)
        shifted = jnp.exp(logits - row_peak)
        totals = jnp.sum(shifted, axis=-1, keepdims=True)
        probs_low = (shifted / totals).astype(jnp.bfloat16)
        log_norm = row_peak + jnp.log(totals)
        heads_out = jnp.einsum(
            "shqk,skd->sqhd", probs_low, values_all, preferred_element_type=jnp.float32
        )
        heads_out = heads_out.reshape(seq_count, span_len, local_heads * head_size).astype(
            jnp.bfloat16
        )
        attn_out = lax.psum(jnp.dot(heads_out, out_w, preferred_element_type=jnp.float32), "tensor")
        residual = source + attn_out
        inv_two = inv_rms(residual)
        normed_two = (residual * inv_two * gain_two).astype(jnp.bfloat16)
        gate_pre = jnp.dot(normed_two, gate_w, preferred_element_type=jnp.float32)
        up_pre = jnp.dot(normed_two, up_w, preferred_element_type=jnp.float32)
        gate_sigmoid = jax.nn.sigmoid(gate_pre)
        silu_gate = gate_pre * gate_sigmoid
        activated = (silu_gate * up_pre).astype(jnp.bfloat16)
        mlp_out = lax.psum(
            jnp.dot(activated, down_w, preferred_element_type=jnp.float32).astype(jnp.bfloat16),
            "tensor",
        ).astype(jnp.float32)
        outputs.append((residual + mlp_out).astype(jnp.bfloat16))
        grad_top = cotangent[row_range]
        grad_list[8] = grad_list[8] + contract(activated, grad_top)
        d_act = project_back(grad_top, down_w)
        d_gate = (d_act * up_pre * gate_sigmoid * (1.0 + gate_pre * (1.0 - gate_sigmoid))).astype(
            jnp.bfloat16
        )
        d_up = (d_act * silu_gate).astype(jnp.bfloat16)
        grad_list[6] = grad_list[6] + contract(normed_two, d_gate)
        grad_list[7] = grad_list[7] + contract(normed_two, d_up)
        mlp_partial = project_back(d_gate, gate_w) + project_back(d_up, up_w)
        d_normed_two = lax.psum(mlp_partial, "tensor")
        d_norm_two, gain_term_two = norm_back(d_normed_two, residual, inv_two, gain_two)
        d_residual = grad_top.astype(jnp.float32) + d_norm_two
        d_residual_low = d_residual.astype(jnp.bfloat16)
        grad_list[5] = grad_list[5] + gain_term_two
        grad_list[4] = grad_list[4] + contract(heads_out, d_residual_low)
        d_heads = project_back(d_residual_low, out_w).astype(jnp.bfloat16)
        d_heads = d_heads.reshape(seq_count, span_len, local_heads, head_size)
        again = (
            jnp.einsum("sqhd,skd->shqk", query_rows, keys_all, preferred_element_type=jnp.float32)
            * score_scale
        )
        again = jnp.where(allowed, again, NEG_FILL)
        probs_again = jnp.exp(again - log_norm)
        probs_again_low = probs_again.astype(jnp.bfloat16)
        d_probs = jnp.einsum(
            "sqhd,skd->shqk", d_heads, values_all, preferred_element_type=jnp.float32
        )
        row_delta = jnp.sum(probs_again * d_probs, axis=-1, keepdims=True)
        d_scores = (probs_again * (d_probs - row_delta)).astype(jnp.bfloat16)
        d_query = (
            jnp.einsum("shqk,skd->sqhd", d_scores, keys_all, preferred_element_type=jnp.float32)
            * score_scale
        )
        key_terms = (
            jnp.einsum("shqk,sqhd->ksd", d_scores, query_rows, preferred_element_type=jnp.float32)
            * score_scale
        )
        value_terms = jnp.einsum(
            "shqk,sqhd->ksd", probs_again_low, d_heads, preferred_element_type=jnp.float32
        )
        kv_terms = jnp.stack([key_terms, value_terms], axis=1).reshape(
            seq_len, 2 * seq_count * head_size
        )
        kv_local = lax.psum_scatter(kv_terms, "ctx", scatter_dimension=0, tiled=True).reshape(
            span_len, 2, seq_count, head_size
        )
        d_key = jnp.transpose(kv_local[:, 0], (1, 0, 2))
        d_value = jnp.transpose(kv_local[:, 1], (1, 0, 2))
        d_query_proj = rotary(d_query, cos_heads, -sin_heads).astype(jnp.bfloat16)
        d_query_proj = d_query_proj.reshape(seq_count, span_len, local_heads * head_size)
        d_key_proj = rotary(d_key, cosine, -sine_table).astype(jnp.bfloat16)
        d_value_proj = d_value.astype(jnp.bfloat16)
        grad_list[1] = grad_list[1] + contract(first_normalized, d_query_proj)
        grad_list[2] = grad_list[2] + contract(first_normalized, d_key_proj)
        grad_list[3] = grad_list[3] + contract(first_normalized, d_value_proj)
        attn_partial = (
            project_back(d_query_proj, query_w)
            + project_back(d_key_proj, key_w)
            + project_back(d_value_proj, value_w)
        )
        d_normed_one = lax.psum(attn_partial, "tensor")
        d_norm_one, gain_term_one = norm_back(d_normed_one, source, inv_one, gain_one)
        grad_list[0] = grad_list[0] + gain_term_one
        input_grads.append(d_residual + d_norm_one)
    input_grad_rows = jnp.concatenate(input_grads, axis=0)
    summed = (
        lax.psum_scatter(grad_list[0], ("dp", "ctx"), scatter_dimension=0, tiled=True),
        lax.psum_scatter(grad_list[1], ("dp", "ctx"), scatter_dimension=0, tiled=True),
        lax.psum_scatter(grad_list[2], ("dp", "ctx"), scatter_dimension=0, tiled=True),
        lax.psum_scatter(grad_list[3], ("dp", "ctx"), scatter_dimension=0, tiled=True),
        lax.psum_scatter(grad_list[4], ("dp", "ctx"), scatter_dimension=1, tiled=True),
        lax.psum_scatter(grad_list[5], ("dp", "ctx"), scatter_dimension=0, tiled=True),
        lax.psum_scatter(grad_list[6], ("dp", "ctx"), scatter_dimension=0, tiled=True),
        lax.psum_scatter(grad_list[7], ("dp", "ctx"), scatter_dimension=0, tiled=True),
        lax.psum_scatter(grad_list[8], ("dp", "ctx"), scatter_dimension=1, tiled=True),
    )
    return (
        jnp.concatenate(outputs, axis=0),
        input_grad_rows,
        summed[0],
        summed[1],
        summed[2],
        summed[3],
        summed[4],
        summed[5],
        summed[6],
        summed[7],
        summed[8],
    )


def solution(mesh):
    in_specs = (
        P("dp", "ctx", None),
        P("dp", "ctx", None),
        P("dp", "ctx"),
        P(("dp", "ctx")),
        P(("dp", "ctx"), "tensor"),
        P(("dp", "ctx"), "tensor"),
        P(("dp", "ctx"), "tensor"),
        P("tensor", ("dp", "ctx")),
        P(("dp", "ctx")),
        P(("dp", "ctx"), "tensor"),
        P(("dp", "ctx"), "tensor"),
        P("tensor", ("dp", "ctx")),
    )
    out_specs = (
        P("dp", "ctx", None),
        P("dp", "ctx", None),
        P(("dp", "ctx")),
        P(("dp", "ctx"), "tensor"),
        P(("dp", "ctx"), "tensor"),
        P(("dp", "ctx"), "tensor"),
        P("tensor", ("dp", "ctx")),
        P(("dp", "ctx")),
        P(("dp", "ctx"), "tensor"),
        P(("dp", "ctx"), "tensor"),
        P("tensor", ("dp", "ctx")),
    )
    return jax.shard_map(
        per_device, mesh=mesh, in_specs=in_specs, out_specs=out_specs, check_vma=False
    )
```

profile of v0, /device:TPU:0, one launch (start us, length us, event | category | flops | bytes accessed | tf_op | source)
XLA Modules:
  0.0 1380.9 jit_solution(2608815866896692798)
XLA Ops:
  11.5 10.4 all-gather.2
  22.0 9.8 all_gather.58
  32.9 9.8 all_gather.55
  43.7 5.1 all_gather.57
  48.7 5.1 all_gather.67
  54.9 5.4 all_gather.68
  60.3 6.0 all_gather.59
  66.3 5.4 all-gather
  71.7 6.1 all-gather.1
  78.5 3.9 copy.47
  95.2 3.8 convolution_bitcast_fusion.1
  102.9 9.4 all-gather.3
  112.3 144.4 %all-reduce.16.cloned.1.call-done = (f32[1,256,2048]{2,1,0:T(8,128)}, f32[1,256,2048]{2,1,0:T(8,128)}) async-done(((f32[1,256,2048]{2,1,0:T(8,128)}, f32[1,256,2048]{2,1,0:T(8,128)}), (f32[1,256,2048]{2,1,0:T(8,128)}, f32[1,256,2048]{2,1,0:T(8,128)})) %all-reduce.16.cloned.1.call-update) | async-done | bytes 4194320 | tf_op jit(solution)/shard_map/psum | solution.py:148
  262.9 37.8 %all-gather.16.cloned.1.call-done = bf16[2048,1408]{1,0:T(8,128)(2,1)} async-done(((bf16[256,1408]{1,0:T(8,128)(2,1)}), bf16[2048,1408]{1,0:T(8,128)(2,1)}) %all-gather.16.cloned.1.call-update) | async-done | bytes 5767184 | tf_op jit(solution)/shard_map/all_gather | solution.py:53
  300.6 5.9 fusion.193
  306.5 39.1 %all-gather.14.cloned.1.call-done = bf16[2048,1408]{1,0:T(8,128)(2,1)} async-done(((bf16[256,1408]{1,0:T(8,128)(2,1)}), bf16[2048,1408]{1,0:T(8,128)(2,1)}) %all-gather.14.cloned.1.call-update) | async-done | bytes 5767184 | tf_op jit(solution)/shard_map/all_gather | solution.py:52
  345.6 6.0 fusion.192
  357.5 34.2 %all-gather.18.cloned.1.call-done = bf16[1408,2048]{1,0:T(8,128)(2,1)} async-done(((bf16[1408,256]{1,0:T(8,128)(2,1)}), bf16[1408,2048]{1,0:T(8,128)(2,1)}) %all-gather.18.cloned.1.call-update) | async-done | bytes 5767184 | tf_op jit(solution)/shard_map/all_gather | solution.py:54
  391.6 7.1 multiply_convert_fusion.2
  399.6 4.6 fusion.198
  404.5 3.7 multiply_convert_fusion.4
  416.5 5.7 fusion.36
  422.2 5.7 fusion.37
  429.2 142.4 %all-reduce.14.cloned.1.call-done = (f32[1,256,2048]{2,1,0:T(8,128)}, f32[1,256,2048]{2,1,0:T(8,128)}) async-done(((f32[1,256,2048]{2,1,0:T(8,128)}, f32[1,256,2048]{2,1,0:T(8,128)}), (f32[1,256,2048]{2,1,0:T(8,128)}, f32[1,256,2048]{2,1,0:T(8,128)})) %all-reduce.14.cloned.1.call-update) | async-done | bytes 4194320 | tf_op jit(solution)/shard_map/psum | solution.py:172
  571.6 5.0 multiply_reduce_fusion.1
  576.6 83.1 %all-reduce.18.cloned.1.call-done = (bf16[1,256,2048]{2,1,0:T(8,128)(2,1)}, bf16[1,256,2048]{2,1,0:T(8,128)(2,1)}) async-done(((bf16[1,256,2048]{2,1,0:T(8,128)(2,1)}, bf16[1,256,2048]{2,1,0:T(8,128)(2,1)}), (bf16[1,256,2048]{2,1,0:T(8,128)(2,1)}, bf16[1,256,2048]{2,1,0:T(8,128)(2,1)})) %all-reduce.18.cloned.1.call-update) | async-done | bytes 2097168 | tf_op jit(solution)/shard_map/psum | solution.py:157
  659.8 7.3 multiply_add_fusion.1
  671.0 5.5 fusion.65
  676.6 8.8 fusion
  688.0 5.7 fusion.62
  693.6 8.9 fusion.3
  707.5 7.0 fusion.16
  728.9 23.7 %reduce-scatter.10.cloned.1.call-done = f32[256,128]{0,1:T(8,128)} async-done(((f32[1024,128]{0,1:T(8,128)}), f32[256,128]{0,1:T(8,128)}) %reduce-scatter.10.cloned.1.call-update) | async-done | bytes 131088 | tf_op jit(solution)/shard_map/reduce_scatter | solution.py:206
  777.1 3.3 fusion.201
  780.4 6.1 convolution_add_fusion.1
  786.7 3.3 fusion.200
  790.0 6.1 convolution_add_fusion.2
  800.3 5.9 convolution_add_fusion
  810.9 105.5 %all-reduce.12.cloned.1.call-done = (f32[1,256,2048]{2,1,0:T(8,128)}, f32[1,256,2048]{2,1,0:T(8,128)}) async-done(((f32[1,256,2048]{2,1,0:T(8,128)}, f32[1,256,2048]{2,1,0:T(8,128)}), (f32[1,256,2048]{2,1,0:T(8,128)}, f32[1,256,2048]{2,1,0:T(8,128)})) %all-reduce.12.cloned.1.call-update) | async-done | bytes 4194320 | tf_op jit(solution)/shard_map/psum | solution.py:223
  916.4 3.3 fusion.43
  919.7 23.9 %all-reduce.2 = (f32[2048]{0:T(1024)S(1)}, f32[2048]{0:T(1024)S(1)}) all-reduce(f32[2048]{0:T(1024)S(1)} %add.260, f32[2048]{0:T(1024)S(1)} %add.265), channel_id=6, replica_groups=mesh['dp'=2,'ctx'=4,'tensor'=4] {'dp','ctx'}, use_global_device_ids=true, to_apply=%region_26.27.clone | all-reduce | flops 4096 | bytes 32768
  944.9 4.5 fusion.42
  953.0 37.8 %reduce-scatter.18.cloned.1.call-done = f32[256,64]{0,1:T(8,128)} async-done(((f32[2048,64]{0,1:T(8,128)}), f32[256,64]{0,1:T(8,128)}) %reduce-scatter.18.cloned.1.call-update) | async-done | bytes 65552 | tf_op jit(solution)/shard_map/reduce_scatter | solution.py:232
  990.8 54.9 %reduce-scatter.20.cloned.1.call-done = f32[512,256]{1,0:T(8,128)} async-done(((f32[512,2048]{1,0:T(8,128)}), f32[512,256]{1,0:T(8,128)}) %reduce-scatter.20.cloned.1.call-update) | async-done | bytes 524304 | tf_op jit(solution)/shard_map/reduce_scatter | solution.py:233
  1045.7 55.0 %reduce-scatter.14.cloned.1.call-done = f32[256,512]{1,0:T(8,128)} async-done(((f32[2048,512]{1,0:T(8,128)}), f32[256,512]{1,0:T(8,128)}) %reduce-scatter.14.cloned.1.call-update) | async-done | bytes 524304 | tf_op jit(solution)/shard_map/reduce_scatter | solution.py:230
  1100.7 91.1 %reduce-scatter.24.cloned.1.call-done = f32[256,1408]{1,0:T(8,128)} async-done(((f32[2048,1408]{1,0:T(8,128)}), f32[256,1408]{1,0:T(8,128)}) %reduce-scatter.24.cloned.1.call-update) | async-done | bytes 1441808 | tf_op jit(solution)/shard_map/reduce_scatter | solution.py:236
  1191.8 91.1 %reduce-scatter.22.cloned.1.call-done = f32[256,1408]{1,0:T(8,128)} async-done(((f32[2048,1408]{1,0:T(8,128)}), f32[256,1408]{1,0:T(8,128)}) %reduce-scatter.22.cloned.1.call-update) | async-done | bytes 1441808 | tf_op jit(solution)/shard_map/reduce_scatter | solution.py:235
  1282.9 90.8 %reduce-scatter.26.cloned.1.call-done = f32[1408,256]{1,0:T(8,128)} async-done(((f32[1408,2048]{1,0:T(8,128)}), f32[1408,256]{1,0:T(8,128)}) %reduce-scatter.26.cloned.1.call-update) | async-done | bytes 1441808 | tf_op jit(solution)/shard_map/reduce_scatter | solution.py:237
  (338 shorter events, 109.7 us)
Async XLA Ops:
  7.2 24.6 %copy-start.2 = (bf16[2,256,2048]{2,1,0:T(8,128)(2,1)S(1)}, bf16[2,256,2048]{2,1,0:T(8,128)(2,1)}, u32[]{:S(2)}) copy-start(bf16[2,256,2048]{2,1,0:T(8,128)(2,1)} %param.12) | copy-start | bytes 6291460
  7.2 14.8 %copy-start.77 = (bf16[256,64]{0,1:T(8,128)(2,1)S(1)}, bf16[256,64]{0,1:T(8,128)(2,1)}, u32[]{:S(2)}) copy-start(bf16[256,64]{0,1:T(8,128)(2,1)} %param.17) | copy-start | bytes 98308
  7.2 71.3 %all-gather.10.cloned.1.call-start = ((), (), s32[]{:S(2)}) async-start(), calls=%async_computation.9 | async-start | bytes 2359296 | tf_op jit(solution)/shard_map/all_gather | solution.py:47
  7.9 87.2 %all-gather.12.cloned.1.call-start = ((), (), s32[]{:S(2)}) async-start(), calls=%async_computation.10 | async-start | bytes 2359296 | tf_op jit(solution)/shard_map/all_gather | solution.py:50
  8.7 248.0 %all-reduce.16.cloned.1.call-start = ((), (), s32[]{:S(2)}) async-start(), calls=%async_computation.25 | async-start | bytes 8388608 | tf_op jit(solution)/shard_map/psum | solution.py:148
  8.7 45.9 %copy-start.85 = (f32[32]{0:T(128)}, f32[32]{0:T(128)S(1)}, u32[]{:S(2)}) copy-start(f32[32]{0:T(128)S(1)} %multiply_power_fusion) | copy-start | bytes 388
  8.8 45.9 %copy-start.83 = (f32[256]{0:T(256)}, f32[256]{0:T(256)S(1)}, u32[]{:S(2)}) copy-start(f32[256]{0:T(256)S(1)} %fusion.169) | copy-start | bytes 3076
  11.5 73.5 %copy-start.79 = (f32[256]{0:T(256)}, f32[256]{0:T(256)S(1)}, u32[]{:S(2)}) copy-start(f32[256]{0:T(256)S(1)} %add_rsqrt_fusion.3) | copy-start | bytes 3076
  11.5 70.9 %copy-start.81 = (f32[256]{0:T(256)}, f32[256]{0:T(256)S(1)}, u32[]{:S(2)}) copy-start(f32[256]{0:T(256)S(1)} %add_rsqrt_fusion.1) | copy-start | bytes 3076
  66.3 19.8 %copy-start.29 = (bf16[1,1024,64]{1,2,0:T(8,128)(2,1)}, bf16[1,1024,64]{1,2,0:T(8,128)(2,1)S(1)}, u32[]{:S(2)}) copy-start(bf16[1,1024,64]{1,2,0:T(8,128)(2,1)S(1)} %all_gather.59) | copy-start | bytes 393220
  71.7 19.5 %copy-start.52 = (bf16[1024,64]{0,1:T(8,128)(2,1)}, bf16[1024,64]{0,1:T(8,128)(2,1)S(1)}, u32[]{:S(2)}) copy-start(bf16[1024,64]{0,1:T(8,128)(2,1)S(1)} %all-gather) | copy-start | bytes 393220
  101.1 199.6 %all-gather.16.cloned.1.call-start = ((), (), s32[]{:S(2)}) async-start(), calls=%async_computation.12 | async-start | bytes 6488064 | tf_op jit(solution)/shard_map/all_gather | solution.py:53
  101.6 243.9 %all-gather.14.cloned.1.call-start = ((), (), s32[]{:S(2)}) async-start(), calls=%async_computation.11 | async-start | bytes 6488064 | tf_op jit(solution)/shard_map/all_gather | solution.py:52
  102.2 289.4 %all-gather.18.cloned.1.call-start = ((), (), s32[]{:S(2)}) async-start(), calls=%async_computation.13 | async-start | bytes 6488064 | tf_op jit(solution)/shard_map/all_gather | solution.py:54
  102.8 468.8 %all-reduce.14.cloned.1.call-start = ((), (), s32[]{:S(2)}) async-start(), calls=%async_computation.24 | async-start | bytes 8388608 | tf_op jit(solution)/shard_map/psum | solution.py:172
  345.6 6.0 copy-start.89
  345.6 8.9 slice-start.6
  391.6 12.6 copy-start.92
  391.6 12.6 copy-start.93
  398.7 14.6 %copy-start.50 = (bf16[256,1408]{1,0:T(8,128)(2,1)}, bf16[256,1408]{1,0:T(8,128)(2,1)S(1)}, u32[]{:S(2)}) copy-start(bf16[256,1408]{1,0:T(8,128)(2,1)S(1)} %get-tuple-element.40) | copy-start | bytes 2162692
  399.6 8.7 slice-start.8
  399.6 10.5 slice-start.4
  416.5 243.3 %all-reduce.18.cloned.1.call-start = ((), (), s32[]{:S(2)}) async-start(), calls=%async_computation.26 | async-start | bytes 4194304 | tf_op jit(solution)/shard_map/psum | solution.py:157
  416.5 5.7 copy-start.18
  427.9 300.2 %reduce-scatter.12.cloned.1.call-start = ((), (), s32[]{:S(2)}) async-start(), calls=%async_computation.15 | async-start | bytes 655360 | tf_op jit(solution)/shard_map/reduce_scatter | solution.py:206
  659.8 8.7 copy-start.8
  676.6 8.8 copy-start.9
  676.6 8.8 copy-start.10
  688.0 14.6 %slice-start = ((s8[8388608]{0:T(1024)(128)(4,1)}), s8[4194304]{0:T(1024)(128)(4,1)S(1)}, s32[]{:S(2)}) async-start(s8[8388608]{0:T(1024)(128)(4,1)} %bitcast.333), calls=%async_computation.27 | async-start | bytes 8388608
  688.0 14.6 %slice-start.2 = ((s8[8388608]{0:T(1024)(128)(4,1)}), s8[4194304]{0:T(1024)(128)(4,1)S(1)}, s32[]{:S(2)}) async-start(s8[8388608]{0:T(1024)(128)(4,1)} %bitcast.335), calls=%async_computation.29 | async-start | bytes 8388608
  693.6 9.0 slice-start.1
  693.6 9.0 slice-start.3
  693.6 9.0 copy-start.59
  693.6 9.0 copy-start.74
  707.2 45.4 %reduce-scatter.10.cloned.1.call-start = ((), (), s32[]{:S(2)}) async-start(), calls=%async_computation.14 | async-start | bytes 655360 | tf_op jit(solution)/shard_map/reduce_scatter | solution.py:206
  707.5 7.0 copy-start.32
  707.5 7.0 copy-start.34
  720.1 196.2 %all-reduce.12.cloned.1.call-start = ((), (), s32[]{:S(2)}) async-start(), calls=%async_computation.23 | async-start | bytes 8388608 | tf_op jit(solution)/shard_map/psum | solution.py:223
  724.2 29.3 %copy-start.84 = (f32[256]{0:T(256)S(1)}, f32[256]{0:T(256)}, u32[]{:S(2)}) copy-start(f32[256]{0:T(256)} %copy-done.83) | copy-start | bytes 3076
  724.2 29.3 %copy-start.86 = (f32[32]{0:T(128)S(1)}, f32[32]{0:T(128)}, u32[]{:S(2)}) copy-start(f32[32]{0:T(128)} %copy-done.85) | copy-start | bytes 388
  724.2 30.2 %copy-start.21 = (bf16[2048,64]{0,1:T(8,128)(2,1)S(1)}, bf16[2048,64]{0,1:T(8,128)(2,1)}, u32[]{:S(2)}) copy-start(bf16[2048,64]{0,1:T(8,128)(2,1)} %copy-done.20) | copy-start | bytes 786436
  761.2 191.8 %reduce-scatter.16.cloned.1.call-start = ((), (), s32[]{:S(2)}) async-start(), calls=%async_computation.17 | async-start | bytes 589824 | tf_op jit(solution)/shard_map/reduce_scatter | solution.py:231
  763.7 227.1 %reduce-scatter.18.cloned.1.call-start = ((), (), s32[]{:S(2)}) async-start(), calls=%async_computation.18 | async-start | bytes 589824 | tf_op jit(solution)/shard_map/reduce_scatter | solution.py:232
  766.4 279.3 %reduce-scatter.20.cloned.1.call-start = ((), (), s32[]{:S(2)}) async-start(), calls=%async_computation.19 | async-start | bytes 4718592 | tf_op jit(solution)/shard_map/reduce_scatter | solution.py:233
  772.0 328.7 %reduce-scatter.14.cloned.1.call-start = ((), (), s32[]{:S(2)}) async-start(), calls=%async_computation.16 | async-start | bytes 4718592 | tf_op jit(solution)/shard_map/reduce_scatter | solution.py:230
  776.8 415.0 %reduce-scatter.24.cloned.1.call-start = ((), (), s32[]{:S(2)}) async-start(), calls=%async_computation.21 | async-start | bytes 12976128 | tf_op jit(solution)/shard_map/reduce_scatter | solution.py:236
  786.6 496.3 %reduce-scatter.22.cloned.1.call-start = ((), (), s32[]{:S(2)}) async-start(), calls=%async_computation.20 | async-start | bytes 12976128 | tf_op jit(solution)/shard_map/reduce_scatter | solution.py:235
  796.1 577.5 %reduce-scatter.26.cloned.1.call-start = ((), (), s32[]{:S(2)}) async-start(), calls=%async_computation.22 | async-start | bytes 12976128 | tf_op jit(solution)/shard_map/reduce_scatter | solution.py:237
  (74 other events, 166.0 us)
Sparse Core Ops, SparseCore 0:
  9.9 31.1 all-gather.9
  43.0 28.4 all-gather.11
  101.2 155.4 all-reduce.15
  258.4 42.1 all-gather.15
  302.4 43.1 all-gather.13
  347.3 44.2 all-gather.17
  416.6 154.9 all-reduce.13
  574.6 85.1 all-reduce.17
  707.4 20.6 reduce-scatter.11
  731.0 21.6 reduce-scatter.9
  761.3 155.0 all-reduce.11
  919.9 33.0 reduce-scatter.15
  956.6 34.1 reduce-scatter.17
  994.6 51.0 reduce-scatter.19
  1049.5 51.1 reduce-scatter.13
  1104.6 87.1 reduce-scatter.23
  1195.7 87.1 reduce-scatter.21
  1286.8 86.8 reduce-scatter.25
where the time goes:
time: 1390 us; the launch traced here: 1380 us
  waiting for transfers between devices  1040 us (75%)
  matrix products  159 us (11%)
  blocking collectives  96.4 us (7%)
  other arithmetic  48.5 us (3%)
  local copies, waits for them, and re-layouts  21.8 us (2%)
  between operations  16.7 us (1%)
    psum x1, waiting for transfers between devices, per_device(): lax.psum(jnp.dot(heads_out, out_w, preferred_element_type=jnp.float32), '...  144 us
    psum x1, waiting for transfers between devices, per_device(): d_normed_two = lax.psum(mlp_partial, 'tensor')  142 us
    psum x1, waiting for transfers between devices, per_device(): d_normed_one = lax.psum(attn_partial, 'tensor')  106 us
    reduce_scatter x1, waiting for transfers between devices, per_device(): lax.psum_scatter(grad_list[7], ('dp', 'ctx'), scatter_dimension=0, tiled=...  91.1 us
    reduce_scatter x1, waiting for transfers between devices, per_device(): lax.psum_scatter(grad_list[6], ('dp', 'ctx'), scatter_dimension=0, tiled=...  91.1 us
    reduce_scatter x1, waiting for transfers between devices, per_device(): lax.psum_scatter(grad_list[8], ('dp', 'ctx'), scatter_dimension=1, tiled=...  90.8 us
    psum x1, waiting for transfers between devices, per_device(): lax.psum(jnp.dot(activated, down_w, preferred_element_type=jnp.float32).a...  83.1 us
    reduce_scatter x1, waiting for transfers between devices, per_device(): lax.psum_scatter(grad_list[1], ('dp', 'ctx'), scatter_dimension=0, tiled=...  55 us
  transfers between devices with their start and end apart: 18, of which 16 were waited for; matrix products, arithmetic and copies ran while one was open for 10% of the time, Pallas kernels for 0%

commit v1 on v0

--- a/solution.py
+++ b/solution.py
@@ -2,6 +2,7 @@
 import jax.numpy as jnp
 from jax import lax
 from jax.sharding import PartitionSpec as P
+from jax.lax import all_gather
 
 MB = 2
 EPSILON = 1e-05
@@ -169,7 +170,12 @@
         grad_list[6] = grad_list[6] + contract(normed_two, d_gate)
         grad_list[7] = grad_list[7] + contract(normed_two, d_up)
         mlp_partial = project_back(d_gate, gate_w) + project_back(d_up, up_w)
-        d_normed_two = lax.psum(mlp_partial, "tensor")
+
+        def mark_face(vec, row_axis):
+            tmp = all_gather(vec, row_axis)
+            return jnp.sum(tmp, 0)
+
+        d_normed_two = mark_face(mlp_partial, row_axis="tensor")
         d_norm_two, gain_term_two = norm_back(d_normed_two, residual, inv_two, gain_two)
         d_residual = grad_top.astype(jnp.float32) + d_norm_two
         d_residual_low = d_residual.astype(jnp.bfloat16)

time: 1390 us -> 1550 us (1.12)
  waiting for transfers between devices: 1040 us -> 1170 us
  other arithmetic: 48.5 us -> 68.3 us
    all_gather x0 -> x2, waiting for transfers between devices: none -> 284 us  [mark_face(): tmp = all_gather(vec, row_axis)]
    psum x1 -> x0, waiting for transfers between devices: 142 us -> none  [per_device(): d_normed_two = lax.psum(mlp_partial, 'tensor')]
  transfers between devices with their start and end apart: 18 -> 19, of which waited for: 16 -> 17; matrix products, arithmetic and copies ran while one was open for 10% -> 9% of each run, Pallas kernels for 0% -> 0%
where the time goes in v1:
time: 1550 us; the launch traced here: 1540 us
  waiting for transfers between devices  1170 us (75%)
  matrix products  164 us (11%)
  blocking collectives  96.6 us (6%)
  other arithmetic  68.3 us (4%)
  local copies, waits for them, and re-layouts  22 us (1%)
  between operations  16.1 us (1%)
    all_gather x2, waiting for transfers between devices, mark_face(): tmp = all_gather(vec, row_axis)  284 us
    psum x1, waiting for transfers between devices, per_device(): lax.psum(jnp.dot(heads_out, out_w, preferred_element_type=jnp.float32), '...  144 us
    psum x1, waiting for transfers between devices, per_device(): d_normed_one = lax.psum(attn_partial, 'tensor')  96.7 us
    reduce_scatter x1, waiting for transfers between devices, per_device(): lax.psum_scatter(grad_list[7], ('dp', 'ctx'), scatter_dimension=0, tiled=...  91.1 us
    reduce_scatter x1, waiting for transfers between devices, per_device(): lax.psum_scatter(grad_list[6], ('dp', 'ctx'), scatter_dimension=0, tiled=...  91.1 us
    reduce_scatter x1, waiting for transfers between devices, per_device(): lax.psum_scatter(grad_list[8], ('dp', 'ctx'), scatter_dimension=1, tiled=...  90.8 us
    psum x1, waiting for transfers between devices, per_device(): lax.psum(jnp.dot(activated, down_w, preferred_element_type=jnp.float32).a...  77.9 us
    reduce_scatter x1, waiting for transfers between devices, per_device(): lax.psum_scatter(grad_list[4], ('dp', 'ctx'), scatter_dimension=1, tiled=...  55.1 us
  transfers between devices with their start and end apart: 19, of which 17 were waited for; matrix products, arithmetic and copies ran while one was open for 9% of the time, Pallas kernels for 0%

profile of v1, /device:TPU:0, one launch (start us, length us, event | category | flops | bytes accessed | tf_op | source)
XLA Modules:
  0.0 1541.1 jit_solution(18199716022214453590)
XLA Ops:
  9.5 10.4 all-gather.4
  22.0 9.8 all_gather.70
  32.9 9.8 all_gather.67
  44.8 5.4 all_gather.80
  50.2 5.1 all_gather.69
  55.3 5.1 all_gather.79
  60.3 6.1 all-gather.1
  66.4 5.5 all_gather.71
  71.9 6.3 all-gather
  103.3 9.2 all-gather.5
  112.6 144.4 %all-reduce.12.cloned.1.call-done = (f32[1,256,2048]{2,1,0:T(8,128)}, f32[1,256,2048]{2,1,0:T(8,128)}) async-done(((f32[1,256,2048]{2,1,0:T(8,128)}, f32[1,256,2048]{2,1,0:T(8,128)}), (f32[1,256,2048]{2,1,0:T(8,128)}, f32[1,256,2048]{2,1,0:T(8,128)})) %all-reduce.12.cloned.1.call-update) | async-done | bytes 4194320 | tf_op jit(solution)/shard_map/psum | solution.py:149
  257.0 4.1 multiply_reduce_fusion.3
  262.7 38.3 %all-gather.18.cloned.1.call-done = bf16[2048,1408]{1,0:T(8,128)(2,1)} async-done(((bf16[256,1408]{1,0:T(8,128)(2,1)}), bf16[2048,1408]{1,0:T(8,128)(2,1)}) %all-gather.18.cloned.1.call-update) | async-done | bytes 5767184 | tf_op jit(solution)/shard_map/all_gather | solution.py:53
  300.9 5.5 fusion.192
  306.5 39.4 %all-gather.20.cloned.1.call-done = bf16[2048,1408]{1,0:T(8,128)(2,1)} async-done(((bf16[256,1408]{1,0:T(8,128)(2,1)}), bf16[2048,1408]{1,0:T(8,128)(2,1)}) %all-gather.20.cloned.1.call-update) | async-done | bytes 5767184 | tf_op jit(solution)/shard_map/all_gather | solution.py:54
  345.9 5.5 fusion.193
  351.4 40.5 %all-gather.22.cloned.1.call-done = bf16[1408,2048]{1,0:T(8,128)(2,1)} async-done(((bf16[1408,256]{1,0:T(8,128)(2,1)}), bf16[1408,2048]{1,0:T(8,128)(2,1)}) %all-gather.22.cloned.1.call-update) | async-done | bytes 5767184 | tf_op jit(solution)/shard_map/all_gather | solution.py:55
  391.9 7.1 multiply_convert_fusion.4
  405.6 149.5 %all-gather.24.cloned.1.call-done = f32[1024,2048]{1,0:T(8,128)} async-done(((f32[256,2048]{1,0:T(8,128)}), f32[1024,2048]{1,0:T(8,128)}) %all-gather.24.cloned.1.call-update) | async-done | bytes 8388624 | tf_op jit(solution)/shard_map/all_gather | solution.py:175
  555.1 5.7 reduce.16
  560.8 4.3 fusion.51
  565.2 4.6 fusion.194
  580.0 5.7 fusion.34
  585.7 6.2 fusion.35
  593.1 134.8 %all-gather.26.cloned.1.call-done = f32[1024,2048]{1,0:T(8,128)} async-done(((f32[256,2048]{1,0:T(8,128)}), f32[1024,2048]{1,0:T(8,128)}) %all-gather.26.cloned.1.call-update) | async-done | bytes 8388624 | tf_op jit(solution)/shard_map/all_gather | solution.py:175
  727.9 5.7 reduce.17
  737.4 77.9 %all-reduce.14.cloned.1.call-done = (bf16[1,256,2048]{2,1,0:T(8,128)(2,1)}, bf16[1,256,2048]{2,1,0:T(8,128)(2,1)}) async-done(((bf16[1,256,2048]{2,1,0:T(8,128)(2,1)}, bf16[1,256,2048]{2,1,0:T(8,128)(2,1)}), (bf16[1,256,2048]{2,1,0:T(8,128)(2,1)}, bf16[1,256,2048]{2,1,0:T(8,128)(2,1)})) %all-reduce.14.cloned.1.call-update) | async-done | bytes 2097168 | tf_op jit(solution)/shard_map/psum | solution.py:158
  815.3 7.3 multiply_add_fusion.1
  826.5 8.7 fusion.3
  835.2 5.6 fusion.62
  843.4 8.9 fusion
  852.3 5.5 fusion.65
  857.9 6.8 fusion.16
  867.8 7.0 fusion.17
  889.2 23.9 %reduce-scatter.12.cloned.1.call-done = f32[256,128]{0,1:T(8,128)} async-done(((f32[1024,128]{0,1:T(8,128)}), f32[256,128]{0,1:T(8,128)}) %reduce-scatter.12.cloned.1.call-update) | async-done | bytes 131088 | tf_op jit(solution)/shard_map/reduce_scatter | solution.py:212
  924.2 7.5 fusion.200
  934.0 10.7 convolution_add_fusion.2
  948.3 6.1 convolution_add_fusion.1
  958.6 5.9 convolution_add_fusion
  980.1 96.7 %all-reduce.10.cloned.1.call-done = (f32[1,256,2048]{2,1,0:T(8,128)}, f32[1,256,2048]{2,1,0:T(8,128)}) async-done(((f32[1,256,2048]{2,1,0:T(8,128)}, f32[1,256,2048]{2,1,0:T(8,128)}), (f32[1,256,2048]{2,1,0:T(8,128)}, f32[1,256,2048]{2,1,0:T(8,128)})) %all-reduce.10.cloned.1.call-update) | async-done | bytes 4194320 | tf_op jit(solution)/shard_map/psum | solution.py:229
  1080.2 23.9 %all-reduce.2 = (f32[2048]{0:T(1024)S(1)}, f32[2048]{0:T(1024)S(1)}) all-reduce(f32[2048]{0:T(1024)S(1)} %add.250, f32[2048]{0:T(1024)S(1)} %add.255), channel_id=8, replica_groups=mesh['dp'=2,'ctx'=4,'tensor'=4] {'dp','ctx'}, use_global_device_ids=true, to_apply=%region_26.27.clone | all-reduce | flops 4096 | bytes 32768
  1105.4 4.5 fusion.40
  1113.7 37.7 %reduce-scatter.18.cloned.1.call-done = f32[256,64]{0,1:T(8,128)} async-done(((f32[2048,64]{0,1:T(8,128)}), f32[256,64]{0,1:T(8,128)}) %reduce-scatter.18.cloned.1.call-update) | async-done | bytes 65552 | tf_op jit(solution)/shard_map/reduce_scatter | solution.py:238
  1151.3 91.1 %reduce-scatter.22.cloned.1.call-done = f32[256,1408]{1,0:T(8,128)} async-done(((f32[2048,1408]{1,0:T(8,128)}), f32[256,1408]{1,0:T(8,128)}) %reduce-scatter.22.cloned.1.call-update) | async-done | bytes 1441808 | tf_op jit(solution)/shard_map/reduce_scatter | solution.py:241
  1242.4 91.1 %reduce-scatter.24.cloned.1.call-done = f32[256,1408]{1,0:T(8,128)} async-done(((f32[2048,1408]{1,0:T(8,128)}), f32[256,1408]{1,0:T(8,128)}) %reduce-scatter.24.cloned.1.call-update) | async-done | bytes 1441808 | tf_op jit(solution)/shard_map/reduce_scatter | solution.py:242
  1333.5 90.8 %reduce-scatter.26.cloned.1.call-done = f32[1408,256]{1,0:T(8,128)} async-done(((f32[1408,2048]{1,0:T(8,128)}), f32[1408,256]{1,0:T(8,128)}) %reduce-scatter.26.cloned.1.call-update) | async-done | bytes 1441808 | tf_op jit(solution)/shard_map/reduce_scatter | solution.py:243
  1424.3 55.0 %reduce-scatter.14.cloned.1.call-done = f32[256,512]{1,0:T(8,128)} async-done(((f32[2048,512]{1,0:T(8,128)}), f32[256,512]{1,0:T(8,128)}) %reduce-scatter.14.cloned.1.call-update) | async-done | bytes 524304 | tf_op jit(solution)/shard_map/reduce_scatter | solution.py:236
  1479.2 55.1 %reduce-scatter.20.cloned.1.call-done = f32[512,256]{1,0:T(8,128)} async-done(((f32[512,2048]{1,0:T(8,128)}), f32[512,256]{1,0:T(8,128)}) %reduce-scatter.20.cloned.1.call-update) | async-done | bytes 524304 | tf_op jit(solution)/shard_map/reduce_scatter | solution.py:239
  (326 shorter events, 123.2 us)
Async XLA Ops:
  7.2 24.7 %copy-start.2 = (bf16[2,256,2048]{2,1,0:T(8,128)(2,1)S(1)}, bf16[2,256,2048]{2,1,0:T(8,128)(2,1)}, u32[]{:S(2)}) copy-start(bf16[2,256,2048]{2,1,0:T(8,128)(2,1)} %param.12) | copy-start | bytes 6291460
  7.2 14.8 copy-start.74
  7.2 71.8 %all-gather.14.cloned.1.call-start = ((), (), s32[]{:S(2)}) async-start(), calls=%async_computation.9 | async-start | bytes 2359296 | tf_op jit(solution)/shard_map/all_gather | solution.py:48
  7.9 87.7 %all-gather.16.cloned.1.call-start = ((), (), s32[]{:S(2)}) async-start(), calls=%async_computation.10 | async-start | bytes 2359296 | tf_op jit(solution)/shard_map/all_gather | solution.py:51
  8.7 248.3 %all-reduce.12.cloned.1.call-start = ((), (), s32[]{:S(2)}) async-start(), calls=%async_computation.26 | async-start | bytes 8388608 | tf_op jit(solution)/shard_map/psum | solution.py:149
  8.7 35.8 %copy-start.83 = (f32[32]{0:T(128)}, f32[32]{0:T(128)S(1)}, u32[]{:S(2)}) copy-start(f32[32]{0:T(128)S(1)} %multiply_power_fusion) | copy-start | bytes 388
  8.8 35.8 %copy-start.81 = (f32[256]{0:T(256)}, f32[256]{0:T(256)S(1)}, u32[]{:S(2)}) copy-start(f32[256]{0:T(256)S(1)} %fusion.169) | copy-start | bytes 3076
  22.0 60.9 %copy-start.77 = (f32[256]{0:T(256)}, f32[256]{0:T(256)S(1)}, u32[]{:S(2)}) copy-start(f32[256]{0:T(256)S(1)} %add_rsqrt_fusion.3) | copy-start | bytes 3076
  22.0 63.4 %copy-start.79 = (f32[256]{0:T(256)}, f32[256]{0:T(256)S(1)}, u32[]{:S(2)}) copy-start(f32[256]{0:T(256)S(1)} %add_rsqrt_fusion.1) | copy-start | bytes 3076
  43.2 7.0 copy-start.85
  66.4 25.2 %copy-start.51 = (bf16[1024,64]{0,1:T(8,128)(2,1)}, bf16[1024,64]{0,1:T(8,128)(2,1)S(1)}, u32[]{:S(2)}) copy-start(bf16[1024,64]{0,1:T(8,128)(2,1)S(1)} %all-gather.1) | copy-start | bytes 393220
  71.9 16.0 %copy-start.29 = (bf16[1,1024,64]{1,2,0:T(8,128)(2,1)}, bf16[1,1024,64]{1,2,0:T(8,128)(2,1)S(1)}, u32[]{:S(2)}) copy-start(bf16[1,1024,64]{1,2,0:T(8,128)(2,1)S(1)} %all_gather.71) | copy-start | bytes 393220
  101.5 199.4 %all-gather.18.cloned.1.call-start = ((), (), s32[]{:S(2)}) async-start(), calls=%async_computation.11 | async-start | bytes 6488064 | tf_op jit(solution)/shard_map/all_gather | solution.py:53
  102.1 243.8 %all-gather.20.cloned.1.call-start = ((), (), s32[]{:S(2)}) async-start(), calls=%async_computation.12 | async-start | bytes 6488064 | tf_op jit(solution)/shard_map/all_gather | solution.py:54
  102.7 289.2 %all-gather.22.cloned.1.call-start = ((), (), s32[]{:S(2)}) async-start(), calls=%async_computation.13 | async-start | bytes 6488064 | tf_op jit(solution)/shard_map/all_gather | solution.py:55
  103.3 451.9 %all-gather.24.cloned.1.call-start = ((), (), s32[]{:S(2)}) async-start(), calls=%async_computation.23 | async-start | bytes 10485760 | tf_op jit(solution)/shard_map/all_gather | solution.py:175
  262.6 83.3 %copy-start.13 = (bf16[256,2048]{1,0:T(8,128)(2,1)}, bf16[256,2048]{1,0:T(8,128)(2,1)S(1)}, u32[]{:S(2)}) copy-start(bf16[256,2048]{1,0:T(8,128)(2,1)S(1)} %fusion.72) | copy-start | bytes 3145732
  391.9 7.1 copy-start.86
  405.4 322.6 %all-gather.26.cloned.1.call-start = ((), (), s32[]{:S(2)}) async-start(), calls=%async_computation.24 | async-start | bytes 10485760 | tf_op jit(solution)/shard_map/all_gather | solution.py:175
  560.8 8.9 slice-start.4
  560.8 10.8 slice-start
  565.1 6.5 slice-start.1
  565.2 9.8 slice-start.2
  580.0 235.3 %all-reduce.14.cloned.1.call-start = ((), (), s32[]{:S(2)}) async-start(), calls=%async_computation.27 | async-start | bytes 4194304 | tf_op jit(solution)/shard_map/psum | solution.py:158
  580.0 5.7 copy-start.18
  592.0 296.4 %reduce-scatter.10.cloned.1.call-start = ((), (), s32[]{:S(2)}) async-start(), calls=%async_computation.14 | async-start | bytes 655360 | tf_op jit(solution)/shard_map/reduce_scatter | solution.py:212
  815.3 8.7 copy-start.7
  826.5 8.7 copy-start.55
  835.2 5.6 copy-start.8
  835.2 5.6 copy-start.10
  852.3 5.5 copy-start.56
  852.3 5.5 copy-start.72
  857.8 6.8 copy-start.36
  857.8 6.8 copy-start.38
  867.5 45.6 %reduce-scatter.12.cloned.1.call-start = ((), (), s32[]{:S(2)}) async-start(), calls=%async_computation.15 | async-start | bytes 655360 | tf_op jit(solution)/shard_map/reduce_scatter | solution.py:212
  867.8 7.0 copy-start.32
  867.8 7.0 copy-start.34
  880.4 196.5 %all-reduce.10.cloned.1.call-start = ((), (), s32[]{:S(2)}) async-start(), calls=%async_computation.25 | async-start | bytes 8388608 | tf_op jit(solution)/shard_map/psum | solution.py:229
  884.4 29.6 %copy-start.82 = (f32[256]{0:T(256)S(1)}, f32[256]{0:T(256)}, u32[]{:S(2)}) copy-start(f32[256]{0:T(256)} %copy-done.81) | copy-start | bytes 3076
  884.4 29.6 %copy-start.84 = (f32[32]{0:T(128)S(1)}, f32[32]{0:T(128)}, u32[]{:S(2)}) copy-start(f32[32]{0:T(128)} %copy-done.83) | copy-start | bytes 388
  884.4 30.4 %copy-start.21 = (bf16[2048,64]{0,1:T(8,128)(2,1)S(1)}, bf16[2048,64]{0,1:T(8,128)(2,1)}, u32[]{:S(2)}) copy-start(bf16[2048,64]{0,1:T(8,128)(2,1)} %copy-done.20) | copy-start | bytes 786436
  921.7 192.0 %reduce-scatter.16.cloned.1.call-start = ((), (), s32[]{:S(2)}) async-start(), calls=%async_computation.17 | async-start | bytes 589824 | tf_op jit(solution)/shard_map/reduce_scatter | solution.py:237
  924.2 227.2 %reduce-scatter.18.cloned.1.call-start = ((), (), s32[]{:S(2)}) async-start(), calls=%async_computation.18 | async-start | bytes 589824 | tf_op jit(solution)/shard_map/reduce_scatter | solution.py:238
  933.9 308.5 %reduce-scatter.22.cloned.1.call-start = ((), (), s32[]{:S(2)}) async-start(), calls=%async_computation.20 | async-start | bytes 12976128 | tf_op jit(solution)/shard_map/reduce_scatter | solution.py:241
  944.7 388.8 %reduce-scatter.24.cloned.1.call-start = ((), (), s32[]{:S(2)}) async-start(), calls=%async_computation.21 | async-start | bytes 12976128 | tf_op jit(solution)/shard_map/reduce_scatter | solution.py:242
  954.4 469.8 %reduce-scatter.26.cloned.1.call-start = ((), (), s32[]{:S(2)}) async-start(), calls=%async_computation.22 | async-start | bytes 12976128 | tf_op jit(solution)/shard_map/reduce_scatter | solution.py:243
  964.6 514.7 %reduce-scatter.14.cloned.1.call-start = ((), (), s32[]{:S(2)}) async-start(), calls=%async_computation.16 | async-start | bytes 4718592 | tf_op jit(solution)/shard_map/reduce_scatter | solution.py:236
  969.3 565.0 %reduce-scatter.20.cloned.1.call-start = ((), (), s32[]{:S(2)}) async-start(), calls=%async_computation.19 | async-start | bytes 4718592 | tf_op jit(solution)/shard_map/reduce_scatter | solution.py:239
  (67 other events, 136.3 us)
Sparse Core Ops, SparseCore 0:
  9.9 31.1 all-gather.13
  43.0 28.4 all-gather.15
  101.6 155.3 all-reduce.11
  258.8 42.1 all-gather.17
  302.7 43.1 all-gather.19
  347.6 44.2 all-gather.21
  405.5 149.5 all-gather.23
  580.1 147.7 all-gather.25
  730.9 84.3 all-reduce.13
  867.7 20.6 reduce-scatter.9
  891.5 21.6 reduce-scatter.11
  921.8 155.0 all-reduce.9
  1080.5 33.0 reduce-scatter.15
  1117.2 34.1 reduce-scatter.17
  1155.2 87.1 reduce-scatter.21
  1246.3 87.1 reduce-scatter.23
  1337.4 86.8 reduce-scatter.25
  1428.1 51.1 reduce-scatter.13
  1483.2 51.0 reduce-scatter.19
